TPU v7x, 256 devices: a whole 4x4x8 slice. The times are simulated.
256 devices in a mesh: ctx: 32 (over z, x_lo, core), head: 8 (over x_hi, y).
Axes of the slice: x: 4 (x_hi: 2, x_lo: 2; x = x_hi * 2 + x_lo), y: 4, z: 8, core: 2. Of those that a mesh axis runs over, the one named last changes fastest.
Arguments:
- block_order: int32 [64], replicated, may hold values from 0 to 63, as said below
- queries: bfloat16 [12288, 4096], P('ctx', 'head'), may hold values from -12 to 12
- key_head_matrix: bfloat16 [12288, 1024], P('ctx', 'head'), may hold values from -6 to 6
- value_head_matrix: bfloat16 [12288, 1024], P('ctx', 'head'), may hold values from -6 to 6
- out_weight: bfloat16 [4096, 4096], P('head'), may hold values from -0.125 to 0.125
- filter_taps: float32 [128, 4096], P(None, 'head'), may hold values from -0.5 to 0.5
- skip_gain: float32 [4096], P('head'), may hold values from 0.5 to 1.5
- gate_values: bfloat16 [12288, 4096], P('ctx', 'head'), may hold values from -4 to 4
Outputs:
- mixed_out: bfloat16 [12288, 4096], P('ctx', 'head')
Inputs may be any that keep to these rules, and one draw needn't show every extreme that they name: A permutation of the 64 sequence blocks; for every d, block_order[2 d] < 32 and block_order[2 d] + block_order[2 d + 1] = 63.
All inputs are finite; a program needn't handle non-finite values.
Results may differ from a plain program's by a relative error of at most 0.015.
Values may be sent and summed in bfloat16 or wider, within the bound.
No kernel may reach another device: no remote copies, remote signals or barrier semaphores. Data moves between devices by JAX's collectives and lax.ppermute only.
A program may use at most 64 MiB of HBM per device.

v0:
```python
import math
import jax
import jax.numpy as jnp
from jax import lax
from jax.sharding import PartitionSpec as P

HEAD_WIDTH = 128
QUERY_PER_KV = 4


def side_by_side(arrays, axis, dim, along):
    widths = [a.shape[along] for a in arrays]
    both = jnp.concatenate(arrays, axis=along)
    out = lax.all_gather(both, axis, axis=dim, tiled=True)
    return tuple(jnp.split(out, [sum(widths[:k]) for k in range(1, len(widths))], axis=along))


def in_blocks(x, dim, size):
    shape = x.shape
    tiles = x.reshape(*shape[:dim], size, shape[dim] // size, *shape[dim + 1 :])
    return jnp.moveaxis(tiles, dim, 0)


def sum_at_owner(x, axis, dim):
    size = lax.axis_size(axis)
    tiles = lax.all_to_all(in_blocks(x, dim, size), axis, 0, 0, tiled=True)
    return jnp.sum(tiles.astype(jnp.float32), axis=0)


def lookup(table_values, index_values):
    matches = jnp.arange(table_values.shape[0], dtype=jnp.int32)[None, :] == index_values[:, None]
    return jnp.sum(jnp.where(matches, table_values[None, :], 0), axis=1)


def shards(
    block_order,
    queries,
    key_head_matrix,
    value_head_matrix,
    out_weight,
    filter_taps,
    skip_gain,
    gate_values,
):
    local_rows = queries.shape[0]
    block_rows = local_rows // 2
    shared_heads = key_head_matrix.shape[1] // HEAD_WIDTH
    position = lax.axis_index("ctx")
    own_blocks = 2 * position + jnp.arange(2, dtype=jnp.int32)
    own_order = lookup(block_order, own_blocks)
    query_place = (
        own_order[:, None] * block_rows + jnp.arange(block_rows, dtype=jnp.int32)[None, :]
    ).reshape(local_rows)
    query_heads = queries.reshape(local_rows, shared_heads, QUERY_PER_KV, HEAD_WIDTH)
    scaling = 1.0 / math.sqrt(HEAD_WIDTH)

    def attend_block(state_now, key_block, value_block, offset):
        running, row_total, summed = state_now
        key_count = key_block.shape[0]
        key_index = offset + jnp.arange(key_count, dtype=jnp.int32)
        key_place = (
            lookup(block_order, key_index // block_rows) * block_rows + key_index % block_rows
        )
        allowed = key_place[None, :] <= query_place[:, None]
        scores = (
            jnp.einsum("qhgd,khd->hgqk", query_heads, key_block, preferred_element_type=jnp.float32)
            * scaling
        )
        scores = jnp.where(allowed, scores, -1e30)
        newest = jnp.maximum(running, jnp.max(scores, axis=-1))
        weight = jnp.where(allowed, jnp.exp(scores - newest[..., None]), 0.0)
        factor = jnp.exp(running - newest)
        row_total = row_total * factor + jnp.sum(weight, axis=-1)
        summed = summed * factor[..., None] + jnp.einsum(
            "hgqk,khd->hgqd",
            weight.astype(jnp.bfloat16),
            value_block,
            preferred_element_type=jnp.float32,
        )
        return (newest, row_total, summed)

    start_state = (
        jnp.full((shared_heads, QUERY_PER_KV, local_rows), -1e30, jnp.float32),
        jnp.zeros((shared_heads, QUERY_PER_KV, local_rows), jnp.float32),
        jnp.zeros((shared_heads, QUERY_PER_KV, local_rows, HEAD_WIDTH), jnp.float32),
    )
    key_piece, value_piece = side_by_side((key_head_matrix, value_head_matrix), "ctx", 0, 1)
    key_count = key_piece.shape[0]
    sub_rows = math.gcd(key_count, 1024)
    steps_count = key_count // sub_rows
    key_split = key_piece.reshape(steps_count, sub_rows, shared_heads, HEAD_WIDTH)
    value_split = value_piece.reshape(steps_count, sub_rows, shared_heads, HEAD_WIDTH)

    def one_step(carried, operands):
        key_block, value_block, block_number = operands
        return (attend_block(carried, key_block, value_block, block_number * sub_rows), None)

    result, unused = lax.scan(
        one_step, start_state, (key_split, value_split, jnp.arange(steps_count, dtype=jnp.int32))
    )
    running, row_total, summed = result
    attended = (
        jnp.transpose(summed / row_total[..., None], (2, 0, 1, 3))
        .reshape(local_rows, -1)
        .astype(jnp.bfloat16)
    )
    partials = jnp.dot(attended, out_weight, preferred_element_type=jnp.float32)
    projected = sum_at_owner(partials.astype(jnp.bfloat16), "head", 1).astype(jnp.bfloat16)
    channels = projected.shape[1]
    reach_rows = filter_taps.shape[0] - 1
    blocks_here = projected.reshape(2, block_rows, channels)
    tail_rows = blocks_here[:, block_rows - reach_rows :, :]
    wanted = own_order - 1
    piece = lax.all_gather(tail_rows, "ctx", axis=0, tiled=True)
    piece_count = piece.shape[0]
    held_blocks = lookup(block_order, jnp.arange(piece_count, dtype=jnp.int32))
    matches = (held_blocks[None, :] == wanted[:, None]).astype(jnp.bfloat16)
    halo_rows = jnp.einsum(
        "sn,nrc->src", matches, piece, preferred_element_type=jnp.float32
    ).astype(jnp.bfloat16)
    extended = jnp.concatenate([halo_rows, blocks_here], axis=1).astype(jnp.float32)
    reversed_taps = jnp.flip(filter_taps, 0)
    kernel = reversed_taps[:, None, :]
    filtered = lax.conv_general_dilated(
        extended,
        kernel,
        (1,),
        "VALID",
        dimension_numbers=("NHC", "HIO", "NHC"),
        feature_group_count=channels,
        precision=lax.Precision.HIGHEST,
    )
    gate_here = gate_values.reshape(2, block_rows, channels).astype(jnp.float32)
    mixed_rows = gate_here * (filtered + skip_gain[None, None, :] * blocks_here.astype(jnp.float32))
    return mixed_rows.reshape(local_rows, channels).astype(jnp.bfloat16)


def solution(mesh):
    return jax.shard_map(
        shards,
        mesh=mesh,
        in_specs=(
            P(),
            P("ctx", "head"),
            P("ctx", "head"),
            P("ctx", "head"),
            P("head", None),
            P(None, "head"),
            P("head"),
            P("ctx", "head"),
        ),
        out_specs=P("ctx", "head"),
        check_vma=False,
    )
```

profile of v0, /device:TPU:1, one launch (start us, length us, event | category | flops | bytes accessed | tf_op | source)
XLA Modules:
  0.0 391.9 jit_solution(11266941806770182200)
XLA Ops:
  10.6 71.8 %all-gather.3.cloned.1.call-done = bf16[12288,256]{1,0:T(8,128)(2,1)} async-done(((bf16[384,256]{1,0:T(8,128)(2,1)}), bf16[12288,256]{1,0:T(8,128)(2,1)}) %all-gather.3.cloned.1.call-update) | async-done | bytes 6291472 | tf_op jit(solution)/shard_map/all_gather | solution.py:14
  82.5 4.7 %fusion.50 = (bf16[12288,128]{1,0:T(8,128)(2,1)}, bf16[12288,128]{1,0:T(8,128)(2,1)}) fusion(bf16[12288,256]{1,0:T(8,128)(2,1)} %all-gather.3.cloned.1.call-done), kind=kLoop, calls=%fused_computation.69 | loop fusion | bytes 12582912 | tf_op jit(solution)/shard_map/split | solution.py:15
  87.2 156.6 %while.17 = (s32[]{:T(128)}, f32[1,4,384]{2,1,0:T(4,128)S(1)}, f32[1,4,384]{2,1,0:T(4,128)S(1)}, f32[1,4,384,128]{3,2,1,0:T(8,128)S(1)}, s32[12]{0:T(128)S(1)}, ...) while((s32[]{:T(128)}, f32[1,4,384]{2,1,0:T(4,128)S(1)}, ...), condition=%wide.region_6.7_spmd.clone, body=%wide.region_2.6_spmd.clone.sunk | while | flops 826960256 | bytes 48233928 | solution.py:98
  89.0 4.8 %fusion.66 = (f32[4,384]{1,0:T(4,128)S(1)}, f32[1024,384,4]{1,0,2:T(8,128)}) fusion(pred[384,1024]{0,1:T(8,128)(4,1)S(1)} %broadcast_compare_fusion.2, bf16[384,1,4,128]{3,0,2,1:T(8,128)(2,1)S(1)} %get-tuple-element.342, bf16[12,1024,1,128]{3,1,2,0:T(8,128)(2,1)} %get-tuple-element.341, s32[]{:T(128)} %get-tuple-element.322), kind=kOutput, calls=%fused_computation.3.clone.1 | convolution fusion | flops 407370240 | bytes 7346688 | tf_op jit(solution)/shard_map/while/body/eval_jaxpr/qhgd,khd->hgqk/dot_general | solution.py:66
  93.8 4.8 %fusion.69 = f32[1,4,384,128]{3,2,1,0:T(8,128)S(1)} fusion(f32[1024,384,4]{1,0,2:T(8,128)} %get-tuple-element.307, f32[4,384]{1,0:T(4,128)S(1)} %bitcast.111, pred[384,1024]{0,1:T(8,128)(4,1)S(1)} %broadcast_compare_fusion.2, f32[1,4,384,128]{3,2,1,0:T(8,128)S(1)} %get-tuple-element.325, f32[4,384]{1,0:T(4,128)S(1)} %get-tuple-element.308, ...), kind=kOutput, calls=%fused_computation.10.clone.1 | convolution fusion | flops 411107328 | bytes 8532481 | tf_op jit(solution)/shard_map/while/body/eval_jaxpr/hgqk,khd->hgqd/dot_general | solution.py:74
  102.1 4.8 %fusion.66 = (f32[4,384]{1,0:T(4,128)S(1)}, f32[1024,384,4]{1,0,2:T(8,128)}) fusion(pred[384,1024]{0,1:T(8,128)(4,1)S(1)} %broadcast_compare_fusion.2, bf16[384,1,4,128]{3,0,2,1:T(8,128)(2,1)S(1)} %get-tuple-element.342, bf16[12,1024,1,128]{3,1,2,0:T(8,128)(2,1)} %get-tuple-element.341, s32[]{:T(128)} %get-tuple-element.322), kind=kOutput, calls=%fused_computation.3.clone.1 | convolution fusion | flops 407370240 | bytes 7346688 | tf_op jit(solution)/shard_map/while/body/eval_jaxpr/qhgd,khd->hgqk/dot_general | solution.py:66
  106.9 4.8 %fusion.69 = f32[1,4,384,128]{3,2,1,0:T(8,128)S(1)} fusion(f32[1024,384,4]{1,0,2:T(8,128)} %get-tuple-element.307, f32[4,384]{1,0:T(4,128)S(1)} %bitcast.111, pred[384,1024]{0,1:T(8,128)(4,1)S(1)} %broadcast_compare_fusion.2, f32[1,4,384,128]{3,2,1,0:T(8,128)S(1)} %get-tuple-element.325, f32[4,384]{1,0:T(4,128)S(1)} %get-tuple-element.308, ...), kind=kOutput, calls=%fused_computation.10.clone.1 | convolution fusion | flops 411107328 | bytes 8532481 | tf_op jit(solution)/shard_map/while/body/eval_jaxpr/hgqk,khd->hgqd/dot_general | solution.py:74
  115.2 4.8 %fusion.66 = (f32[4,384]{1,0:T(4,128)S(1)}, f32[1024,384,4]{1,0,2:T(8,128)}) fusion(pred[384,1024]{0,1:T(8,128)(4,1)S(1)} %broadcast_compare_fusion.2, bf16[384,1,4,128]{3,0,2,1:T(8,128)(2,1)S(1)} %get-tuple-element.342, bf16[12,1024,1,128]{3,1,2,0:T(8,128)(2,1)} %get-tuple-element.341, s32[]{:T(128)} %get-tuple-element.322), kind=kOutput, calls=%fused_computation.3.clone.1 | convolution fusion | flops 407370240 | bytes 7346688 | tf_op jit(solution)/shard_map/while/body/eval_jaxpr/qhgd,khd->hgqk/dot_general | solution.py:66
  120.0 4.8 %fusion.69 = f32[1,4,384,128]{3,2,1,0:T(8,128)S(1)} fusion(f32[1024,384,4]{1,0,2:T(8,128)} %get-tuple-element.307, f32[4,384]{1,0:T(4,128)S(1)} %bitcast.111, pred[384,1024]{0,1:T(8,128)(4,1)S(1)} %broadcast_compare_fusion.2, f32[1,4,384,128]{3,2,1,0:T(8,128)S(1)} %get-tuple-element.325, f32[4,384]{1,0:T(4,128)S(1)} %get-tuple-element.308, ...), kind=kOutput, calls=%fused_computation.10.clone.1 | convolution fusion | flops 411107328 | bytes 8532481 | tf_op jit(solution)/shard_map/while/body/eval_jaxpr/hgqk,khd->hgqd/dot_general | solution.py:74
  128.2 4.8 %fusion.66 = (f32[4,384]{1,0:T(4,128)S(1)}, f32[1024,384,4]{1,0,2:T(8,128)}) fusion(pred[384,1024]{0,1:T(8,128)(4,1)S(1)} %broadcast_compare_fusion.2, bf16[384,1,4,128]{3,0,2,1:T(8,128)(2,1)S(1)} %get-tuple-element.342, bf16[12,1024,1,128]{3,1,2,0:T(8,128)(2,1)} %get-tuple-element.341, s32[]{:T(128)} %get-tuple-element.322), kind=kOutput, calls=%fused_computation.3.clone.1 | convolution fusion | flops 407370240 | bytes 7346688 | tf_op jit(solution)/shard_map/while/body/eval_jaxpr/qhgd,khd->hgqk/dot_general | solution.py:66
  133.0 4.8 %fusion.69 = f32[1,4,384,128]{3,2,1,0:T(8,128)S(1)} fusion(f32[1024,384,4]{1,0,2:T(8,128)} %get-tuple-element.307, f32[4,384]{1,0:T(4,128)S(1)} %bitcast.111, pred[384,1024]{0,1:T(8,128)(4,1)S(1)} %broadcast_compare_fusion.2, f32[1,4,384,128]{3,2,1,0:T(8,128)S(1)} %get-tuple-element.325, f32[4,384]{1,0:T(4,128)S(1)} %get-tuple-element.308, ...), kind=kOutput, calls=%fused_computation.10.clone.1 | convolution fusion | flops 411107328 | bytes 8532481 | tf_op jit(solution)/shard_map/while/body/eval_jaxpr/hgqk,khd->hgqd/dot_general | solution.py:74
  141.3 4.8 %fusion.66 = (f32[4,384]{1,0:T(4,128)S(1)}, f32[1024,384,4]{1,0,2:T(8,128)}) fusion(pred[384,1024]{0,1:T(8,128)(4,1)S(1)} %broadcast_compare_fusion.2, bf16[384,1,4,128]{3,0,2,1:T(8,128)(2,1)S(1)} %get-tuple-element.342, bf16[12,1024,1,128]{3,1,2,0:T(8,128)(2,1)} %get-tuple-element.341, s32[]{:T(128)} %get-tuple-element.322), kind=kOutput, calls=%fused_computation.3.clone.1 | convolution fusion | flops 407370240 | bytes 7346688 | tf_op jit(solution)/shard_map/while/body/eval_jaxpr/qhgd,khd->hgqk/dot_general | solution.py:66
  146.1 4.8 %fusion.69 = f32[1,4,384,128]{3,2,1,0:T(8,128)S(1)} fusion(f32[1024,384,4]{1,0,2:T(8,128)} %get-tuple-element.307, f32[4,384]{1,0:T(4,128)S(1)} %bitcast.111, pred[384,1024]{0,1:T(8,128)(4,1)S(1)} %broadcast_compare_fusion.2, f32[1,4,384,128]{3,2,1,0:T(8,128)S(1)} %get-tuple-element.325, f32[4,384]{1,0:T(4,128)S(1)} %get-tuple-element.308, ...), kind=kOutput, calls=%fused_computation.10.clone.1 | convolution fusion | flops 411107328 | bytes 8532481 | tf_op jit(solution)/shard_map/while/body/eval_jaxpr/hgqk,khd->hgqd/dot_general | solution.py:74
  154.3 4.8 %fusion.66 = (f32[4,384]{1,0:T(4,128)S(1)}, f32[1024,384,4]{1,0,2:T(8,128)}) fusion(pred[384,1024]{0,1:T(8,128)(4,1)S(1)} %broadcast_compare_fusion.2, bf16[384,1,4,128]{3,0,2,1:T(8,128)(2,1)S(1)} %get-tuple-element.342, bf16[12,1024,1,128]{3,1,2,0:T(8,128)(2,1)} %get-tuple-element.341, s32[]{:T(128)} %get-tuple-element.322), kind=kOutput, calls=%fused_computation.3.clone.1 | convolution fusion | flops 407370240 | bytes 7346688 | tf_op jit(solution)/shard_map/while/body/eval_jaxpr/qhgd,khd->hgqk/dot_general | solution.py:66
  159.1 4.8 %fusion.69 = f32[1,4,384,128]{3,2,1,0:T(8,128)S(1)} fusion(f32[1024,384,4]{1,0,2:T(8,128)} %get-tuple-element.307, f32[4,384]{1,0:T(4,128)S(1)} %bitcast.111, pred[384,1024]{0,1:T(8,128)(4,1)S(1)} %broadcast_compare_fusion.2, f32[1,4,384,128]{3,2,1,0:T(8,128)S(1)} %get-tuple-element.325, f32[4,384]{1,0:T(4,128)S(1)} %get-tuple-element.308, ...), kind=kOutput, calls=%fused_computation.10.clone.1 | convolution fusion | flops 411107328 | bytes 8532481 | tf_op jit(solution)/shard_map/while/body/eval_jaxpr/hgqk,khd->hgqd/dot_general | solution.py:74
  167.4 4.8 %fusion.66 = (f32[4,384]{1,0:T(4,128)S(1)}, f32[1024,384,4]{1,0,2:T(8,128)}) fusion(pred[384,1024]{0,1:T(8,128)(4,1)S(1)} %broadcast_compare_fusion.2, bf16[384,1,4,128]{3,0,2,1:T(8,128)(2,1)S(1)} %get-tuple-element.342, bf16[12,1024,1,128]{3,1,2,0:T(8,128)(2,1)} %get-tuple-element.341, s32[]{:T(128)} %get-tuple-element.322), kind=kOutput, calls=%fused_computation.3.clone.1 | convolution fusion | flops 407370240 | bytes 7346688 | tf_op jit(solution)/shard_map/while/body/eval_jaxpr/qhgd,khd->hgqk/dot_general | solution.py:66
  172.2 4.8 %fusion.69 = f32[1,4,384,128]{3,2,1,0:T(8,128)S(1)} fusion(f32[1024,384,4]{1,0,2:T(8,128)} %get-tuple-element.307, f32[4,384]{1,0:T(4,128)S(1)} %bitcast.111, pred[384,1024]{0,1:T(8,128)(4,1)S(1)} %broadcast_compare_fusion.2, f32[1,4,384,128]{3,2,1,0:T(8,128)S(1)} %get-tuple-element.325, f32[4,384]{1,0:T(4,128)S(1)} %get-tuple-element.308, ...), kind=kOutput, calls=%fused_computation.10.clone.1 | convolution fusion | flops 411107328 | bytes 8532481 | tf_op jit(solution)/shard_map/while/body/eval_jaxpr/hgqk,khd->hgqd/dot_general | solution.py:74
  180.4 4.8 %fusion.66 = (f32[4,384]{1,0:T(4,128)S(1)}, f32[1024,384,4]{1,0,2:T(8,128)}) fusion(pred[384,1024]{0,1:T(8,128)(4,1)S(1)} %broadcast_compare_fusion.2, bf16[384,1,4,128]{3,0,2,1:T(8,128)(2,1)S(1)} %get-tuple-element.342, bf16[12,1024,1,128]{3,1,2,0:T(8,128)(2,1)} %get-tuple-element.341, s32[]{:T(128)} %get-tuple-element.322), kind=kOutput, calls=%fused_computation.3.clone.1 | convolution fusion | flops 407370240 | bytes 7346688 | tf_op jit(solution)/shard_map/while/body/eval_jaxpr/qhgd,khd->hgqk/dot_general | solution.py:66
  185.2 4.8 %fusion.69 = f32[1,4,384,128]{3,2,1,0:T(8,128)S(1)} fusion(f32[1024,384,4]{1,0,2:T(8,128)} %get-tuple-element.307, f32[4,384]{1,0:T(4,128)S(1)} %bitcast.111, pred[384,1024]{0,1:T(8,128)(4,1)S(1)} %broadcast_compare_fusion.2, f32[1,4,384,128]{3,2,1,0:T(8,128)S(1)} %get-tuple-element.325, f32[4,384]{1,0:T(4,128)S(1)} %get-tuple-element.308, ...), kind=kOutput, calls=%fused_computation.10.clone.1 | convolution fusion | flops 411107328 | bytes 8532481 | tf_op jit(solution)/shard_map/while/body/eval_jaxpr/hgqk,khd->hgqd/dot_general | solution.py:74
  193.5 4.8 %fusion.66 = (f32[4,384]{1,0:T(4,128)S(1)}, f32[1024,384,4]{1,0,2:T(8,128)}) fusion(pred[384,1024]{0,1:T(8,128)(4,1)S(1)} %broadcast_compare_fusion.2, bf16[384,1,4,128]{3,0,2,1:T(8,128)(2,1)S(1)} %get-tuple-element.342, bf16[12,1024,1,128]{3,1,2,0:T(8,128)(2,1)} %get-tuple-element.341, s32[]{:T(128)} %get-tuple-element.322), kind=kOutput, calls=%fused_computation.3.clone.1 | convolution fusion | flops 407370240 | bytes 7346688 | tf_op jit(solution)/shard_map/while/body/eval_jaxpr/qhgd,khd->hgqk/dot_general | solution.py:66
  198.3 4.8 %fusion.69 = f32[1,4,384,128]{3,2,1,0:T(8,128)S(1)} fusion(f32[1024,384,4]{1,0,2:T(8,128)} %get-tuple-element.307, f32[4,384]{1,0:T(4,128)S(1)} %bitcast.111, pred[384,1024]{0,1:T(8,128)(4,1)S(1)} %broadcast_compare_fusion.2, f32[1,4,384,128]{3,2,1,0:T(8,128)S(1)} %get-tuple-element.325, f32[4,384]{1,0:T(4,128)S(1)} %get-tuple-element.308, ...), kind=kOutput, calls=%fused_computation.10.clone.1 | convolution fusion | flops 411107328 | bytes 8532481 | tf_op jit(solution)/shard_map/while/body/eval_jaxpr/hgqk,khd->hgqd/dot_general | solution.py:74
  206.5 4.8 %fusion.66 = (f32[4,384]{1,0:T(4,128)S(1)}, f32[1024,384,4]{1,0,2:T(8,128)}) fusion(pred[384,1024]{0,1:T(8,128)(4,1)S(1)} %broadcast_compare_fusion.2, bf16[384,1,4,128]{3,0,2,1:T(8,128)(2,1)S(1)} %get-tuple-element.342, bf16[12,1024,1,128]{3,1,2,0:T(8,128)(2,1)} %get-tuple-element.341, s32[]{:T(128)} %get-tuple-element.322), kind=kOutput, calls=%fused_computation.3.clone.1 | convolution fusion | flops 407370240 | bytes 7346688 | tf_op jit(solution)/shard_map/while/body/eval_jaxpr/qhgd,khd->hgqk/dot_general | solution.py:66
  211.3 4.8 %fusion.69 = f32[1,4,384,128]{3,2,1,0:T(8,128)S(1)} fusion(f32[1024,384,4]{1,0,2:T(8,128)} %get-tuple-element.307, f32[4,384]{1,0:T(4,128)S(1)} %bitcast.111, pred[384,1024]{0,1:T(8,128)(4,1)S(1)} %broadcast_compare_fusion.2, f32[1,4,384,128]{3,2,1,0:T(8,128)S(1)} %get-tuple-element.325, f32[4,384]{1,0:T(4,128)S(1)} %get-tuple-element.308, ...), kind=kOutput, calls=%fused_computation.10.clone.1 | convolution fusion | flops 411107328 | bytes 8532481 | tf_op jit(solution)/shard_map/while/body/eval_jaxpr/hgqk,khd->hgqd/dot_general | solution.py:74
  219.6 4.8 %fusion.66 = (f32[4,384]{1,0:T(4,128)S(1)}, f32[1024,384,4]{1,0,2:T(8,128)}) fusion(pred[384,1024]{0,1:T(8,128)(4,1)S(1)} %broadcast_compare_fusion.2, bf16[384,1,4,128]{3,0,2,1:T(8,128)(2,1)S(1)} %get-tuple-element.342, bf16[12,1024,1,128]{3,1,2,0:T(8,128)(2,1)} %get-tuple-element.341, s32[]{:T(128)} %get-tuple-element.322), kind=kOutput, calls=%fused_computation.3.clone.1 | convolution fusion | flops 407370240 | bytes 7346688 | tf_op jit(solution)/shard_map/while/body/eval_jaxpr/qhgd,khd->hgqk/dot_general | solution.py:66
  224.4 4.8 %fusion.69 = f32[1,4,384,128]{3,2,1,0:T(8,128)S(1)} fusion(f32[1024,384,4]{1,0,2:T(8,128)} %get-tuple-element.307, f32[4,384]{1,0:T(4,128)S(1)} %bitcast.111, pred[384,1024]{0,1:T(8,128)(4,1)S(1)} %broadcast_compare_fusion.2, f32[1,4,384,128]{3,2,1,0:T(8,128)S(1)} %get-tuple-element.325, f32[4,384]{1,0:T(4,128)S(1)} %get-tuple-element.308, ...), kind=kOutput, calls=%fused_computation.10.clone.1 | convolution fusion | flops 411107328 | bytes 8532481 | tf_op jit(solution)/shard_map/while/body/eval_jaxpr/hgqk,khd->hgqd/dot_general | solution.py:74
  232.6 4.8 %fusion.66 = (f32[4,384]{1,0:T(4,128)S(1)}, f32[1024,384,4]{1,0,2:T(8,128)}) fusion(pred[384,1024]{0,1:T(8,128)(4,1)S(1)} %broadcast_compare_fusion.2, bf16[384,1,4,128]{3,0,2,1:T(8,128)(2,1)S(1)} %get-tuple-element.342, bf16[12,1024,1,128]{3,1,2,0:T(8,128)(2,1)} %get-tuple-element.341, s32[]{:T(128)} %get-tuple-element.322), kind=kOutput, calls=%fused_computation.3.clone.1 | convolution fusion | flops 407370240 | bytes 7346688 | tf_op jit(solution)/shard_map/while/body/eval_jaxpr/qhgd,khd->hgqk/dot_general | solution.py:66
  237.4 4.8 %fusion.69 = f32[1,4,384,128]{3,2,1,0:T(8,128)S(1)} fusion(f32[1024,384,4]{1,0,2:T(8,128)} %get-tuple-element.307, f32[4,384]{1,0:T(4,128)S(1)} %bitcast.111, pred[384,1024]{0,1:T(8,128)(4,1)S(1)} %broadcast_compare_fusion.2, f32[1,4,384,128]{3,2,1,0:T(8,128)S(1)} %get-tuple-element.325, f32[4,384]{1,0:T(4,128)S(1)} %get-tuple-element.308, ...), kind=kOutput, calls=%fused_computation.10.clone.1 | convolution fusion | flops 411107328 | bytes 8532481 | tf_op jit(solution)/shard_map/while/body/eval_jaxpr/hgqk,khd->hgqd/dot_general | solution.py:74
  244.2 4.0 %convolution_convert_fusion = bf16[384,4096]{1,0:T(8,128)(2,1)S(1)} fusion(bf16[384,512]{0,1:T(8,128)(2,1)S(1)} %bitcast.114, bf16[512,4096]{1,0:T(8,128)(2,1)} %param.14), kind=kOutput, calls=%fused_computation.44 | convolution fusion | flops 1612185600 | bytes 7733248 | tf_op jit(solution)/shard_map/dot_general | solution.py:107
  248.5 44.2 %all_to_all.5 = bf16[8,384,512]{2,1,0:T(8,128)(2,1)S(1)} all-to-all(bf16[8,384,512]{2,1,0:T(8,128)(2,1)S(1)} %bitcast.104), channel_id=1, replica_groups=mesh['ctx'=32,'head'=8] {'head'}, dimensions={0} | all-to-all | bytes 6291456 | tf_op jit(solution)/shard_map/all_to_all | solution.py:26
  296.5 67.8 %all-gather.5.cloned.1.call-done = bf16[64,127,512]{2,1,0:T(8,128)(2,1)} async-done(((bf16[2,127,512]{2,1,0:T(8,128)(2,1)}), bf16[64,127,512]{2,1,0:T(8,128)(2,1)}) %all-gather.5.cloned.1.call-update) | async-done | bytes 8323088 | tf_op jit(solution)/shard_map/all_gather | solution.py:114
  364.3 12.2 %fusion.35 = bf16[2,127,512]{2,0,1:T(2,128)(2,1)S(1)} fusion(bf16[64,127,512]{2,1,0:T(8,128)(2,1)} %all-gather.5.cloned.1.call-done, s32[64]{0:T(128)S(1)} %select_reduce_fusion.1, s32[2]{0:T(128)S(1)} %get-tuple-element.238), kind=kOutput, calls=%fused_computation.46 | convolution fusion | flops 16776320 | bytes 8583432 | tf_op jit(solution)/shard_map/sn,nrc->src/dot_general | solution.py:118
  376.5 7.5 %fusion.39 = f32[2,192,512]{2,0,1:T(2,128)S(1)} fusion(bf16[2,192,512]{2,0,1:T(2,128)(2,1)S(1)} %copy.49, bf16[2,127,512]{2,0,1:T(2,128)(2,1)S(1)} %fusion.35, f32[128,1,512]{2,0,1:T(8,128)S(1)} %bitcast.116), kind=kOutput, calls=%fused_computation.51 | convolution fusion | flops 303296512 | bytes 1701888 | tf_op jit(solution)/shard_map/conv_general_dilated | solution.py:124
  (185 shorter events, 42.2 us)
Async XLA Ops:
  6.5 75.9 %all-gather.3.cloned.1.call-start = ((), (), s32[]{:S(2)}) async-start(), calls=%async_computation.1 | async-start | bytes 6488064 | tf_op jit(solution)/shard_map/all_gather | solution.py:14
  8.2 356.1 %all-gather.5.cloned.1.call-start = ((), (), s32[]{:S(2)}) async-start(), calls=%async_computation.2 | async-start | bytes 8650752 | tf_op jit(solution)/shard_map/all_gather | solution.py:114
  10.6 76.6 %copy-start.2 = (s32[64]{0:T(128)S(1)}, s32[64]{0:T(128)}, u32[]{:S(2)}) copy-start(s32[64]{0:T(128)} %param.10) | copy-start | bytes 772
  93.8 4.8 %copy-start = (f32[1024,384,4]{1,0,2:T(8,128)S(1)}, f32[1024,384,4]{1,0,2:T(8,128)}, u32[]{:S(2)}) copy-start(f32[1024,384,4]{1,0,2:T(8,128)} %get-tuple-element.307) | copy-start | bytes 18874372 | tf_op jit(solution)/shard_map/while
  106.9 4.8 %copy-start = (f32[1024,384,4]{1,0,2:T(8,128)S(1)}, f32[1024,384,4]{1,0,2:T(8,128)}, u32[]{:S(2)}) copy-start(f32[1024,384,4]{1,0,2:T(8,128)} %get-tuple-element.307) | copy-start | bytes 18874372 | tf_op jit(solution)/shard_map/while
  119.9 4.8 %copy-start = (f32[1024,384,4]{1,0,2:T(8,128)S(1)}, f32[1024,384,4]{1,0,2:T(8,128)}, u32[]{:S(2)}) copy-start(f32[1024,384,4]{1,0,2:T(8,128)} %get-tuple-element.307) | copy-start | bytes 18874372 | tf_op jit(solution)/shard_map/while
  133.0 4.8 %copy-start = (f32[1024,384,4]{1,0,2:T(8,128)S(1)}, f32[1024,384,4]{1,0,2:T(8,128)}, u32[]{:S(2)}) copy-start(f32[1024,384,4]{1,0,2:T(8,128)} %get-tuple-element.307) | copy-start | bytes 18874372 | tf_op jit(solution)/shard_map/while
  146.0 4.8 %copy-start = (f32[1024,384,4]{1,0,2:T(8,128)S(1)}, f32[1024,384,4]{1,0,2:T(8,128)}, u32[]{:S(2)}) copy-start(f32[1024,384,4]{1,0,2:T(8,128)} %get-tuple-element.307) | copy-start | bytes 18874372 | tf_op jit(solution)/shard_map/while
  159.1 4.8 %copy-start = (f32[1024,384,4]{1,0,2:T(8,128)S(1)}, f32[1024,384,4]{1,0,2:T(8,128)}, u32[]{:S(2)}) copy-start(f32[1024,384,4]{1,0,2:T(8,128)} %get-tuple-element.307) | copy-start | bytes 18874372 | tf_op jit(solution)/shard_map/while
  172.2 4.8 %copy-start = (f32[1024,384,4]{1,0,2:T(8,128)S(1)}, f32[1024,384,4]{1,0,2:T(8,128)}, u32[]{:S(2)}) copy-start(f32[1024,384,4]{1,0,2:T(8,128)} %get-tuple-element.307) | copy-start | bytes 18874372 | tf_op jit(solution)/shard_map/while
  185.2 4.8 %copy-start = (f32[1024,384,4]{1,0,2:T(8,128)S(1)}, f32[1024,384,4]{1,0,2:T(8,128)}, u32[]{:S(2)}) copy-start(f32[1024,384,4]{1,0,2:T(8,128)} %get-tuple-element.307) | copy-start | bytes 18874372 | tf_op jit(solution)/shard_map/while
  198.3 4.8 %copy-start = (f32[1024,384,4]{1,0,2:T(8,128)S(1)}, f32[1024,384,4]{1,0,2:T(8,128)}, u32[]{:S(2)}) copy-start(f32[1024,384,4]{1,0,2:T(8,128)} %get-tuple-element.307) | copy-start | bytes 18874372 | tf_op jit(solution)/shard_map/while
  211.3 4.8 %copy-start = (f32[1024,384,4]{1,0,2:T(8,128)S(1)}, f32[1024,384,4]{1,0,2:T(8,128)}, u32[]{:S(2)}) copy-start(f32[1024,384,4]{1,0,2:T(8,128)} %get-tuple-element.307) | copy-start | bytes 18874372 | tf_op jit(solution)/shard_map/while
  224.4 4.8 %copy-start = (f32[1024,384,4]{1,0,2:T(8,128)S(1)}, f32[1024,384,4]{1,0,2:T(8,128)}, u32[]{:S(2)}) copy-start(f32[1024,384,4]{1,0,2:T(8,128)} %get-tuple-element.307) | copy-start | bytes 18874372 | tf_op jit(solution)/shard_map/while
  237.4 4.8 %copy-start = (f32[1024,384,4]{1,0,2:T(8,128)S(1)}, f32[1024,384,4]{1,0,2:T(8,128)}, u32[]{:S(2)}) copy-start(f32[1024,384,4]{1,0,2:T(8,128)} %get-tuple-element.307) | copy-start | bytes 18874372 | tf_op jit(solution)/shard_map/while
  376.5 7.5 %copy-start.1 = (bf16[384,512]{1,0:T(8,128)(2,1)S(1)}, bf16[384,512]{1,0:T(8,128)(2,1)}, u32[]{:S(2)}) copy-start(bf16[384,512]{1,0:T(8,128)(2,1)} %param.17) | copy-start | bytes 1179652
  376.5 7.5 %copy-start.3 = (f32[512]{0:T(512)S(1)}, f32[512]{0:T(512)}, u32[]{:S(2)}) copy-start(f32[512]{0:T(512)} %param.16) | copy-start | bytes 6148
Sparse Core Ops, SparseCore 0:
  9.2 73.2 all-gather.2
  294.3 69.9 all-gather.4
where the time goes:
time: 393 us; the launch traced here: 392 us
  waiting for transfers between devices  140 us (36%)
  matrix products  139 us (35%)
  blocking collectives  44.2 us (11%)
  other arithmetic  29.1 us (7%)
  local copies, waits for them, and re-layouts  17.8 us (5%)
  between operations  13.5 us (3%)
  loops' own time  8.67 us (2%)
    all_gather x1, waiting for transfers between devices, side_by_side(): out = lax.all_gather(both, axis, axis=dim, tiled=True)  71.8 us
    all_gather x1, waiting for transfers between devices, shards(): piece = lax.all_gather(tail_rows, 'ctx', axis=0, tiled=True)  67.8 us
    dot_general x12, matrix products, attend_block(): jnp.einsum('hgqk,khd->hgqd', weight.astype(jnp.bfloat16), value_block, pr...  57.8 us
    dot_general x12, matrix products, attend_block(): jnp.einsum('qhgd,khd->hgqk', query_heads, key_block, preferred_element_ty...  57.3 us
    all_to_all x1, blocking collectives, sum_at_owner(): tiles = lax.all_to_all(in_blocks(x, dim, size), axis, 0, 0, tiled=True)  44.2 us
    reduce_sum x12, other arithmetic, attend_block(): row_total = row_total * factor + jnp.sum(weight, axis=-1)  18.6 us
    dot_general x1, matrix products, shards(): jnp.einsum('sn,nrc->src', matches, piece, preferred_element_type=jnp.floa...  12.2 us
    another operation x1, loops' own time, shards(): lax.scan(one_step, start_state, (key_split, value_split, jnp.arange(steps...  8.67 us
  transfers between devices with their start and end apart: 2, of which 2 were waited for; matrix products, arithmetic and copies ran while one was open for 1% of the time, Pallas kernels for 0%

commit v1 on v0

--- a/solution.py
+++ b/solution.py
@@ -111,7 +111,9 @@
     blocks_here = projected.reshape(2, block_rows, channels)
     tail_rows = blocks_here[:, block_rows - reach_rows :, :]
     wanted = own_order - 1
-    piece = lax.all_gather(tail_rows, "ctx", axis=0, tiled=True)
+    piece = jnp.concatenate(
+        lax.all_to_all(jnp.stack([tail_rows] * lax.axis_size("ctx")), "ctx", 0, 0), axis=0
+    )
     piece_count = piece.shape[0]
     held_blocks = lookup(block_order, jnp.arange(piece_count, dtype=jnp.int32))
     matches = (held_blocks[None, :] == wanted[:, None]).astype(jnp.bfloat16)

time: 393 us -> 540 us (1.37)
  waiting for transfers between devices: 140 us -> 256 us
  local copies, waits for them, and re-layouts: 17.8 us -> 47.2 us
  starting transfers between devices: 0.04 us -> 8.44 us
  matrix products: 139 us -> 131 us
    all_to_all x0 -> x1, waiting for transfers between devices: none -> 184 us  [shards(): lax.all_to_all(jnp.stack([tail_rows] * lax.axis_size('ctx')), 'ctx', 0, 0)]
    all_gather x1 -> x0, waiting for transfers between devices: 67.8 us -> none  [shards(): piece = lax.all_gather(tail_rows, 'ctx', axis=0, tiled=True)]
    reshape x0 -> x1, local copies, waits for them, and re-layouts: none -> 17.8 us  [shards(): jnp.concatenate(lax.all_to_all(jnp.stack([tail_rows] * lax.axis_size('ctx...]
    all_to_all x0 -> x1, starting transfers between devices: none -> 8.44 us  [shards(): lax.all_to_all(jnp.stack([tail_rows] * lax.axis_size('ctx')), 'ctx', 0, 0)]
    all_to_all x0 -> x1, local copies, waits for them, and re-layouts: none -> 8.05 us  [shards(): lax.all_to_all(jnp.stack([tail_rows] * lax.axis_size('ctx')), 'ctx', 0, 0)]
    dot_general x1, matrix products: 12.2 us -> 4.6 us  [shards(): jnp.einsum('sn,nrc->src', matches, piece, preferred_element_type=jnp.floa...]
    another operation x0 -> x1, local copies, waits for them, and re-layouts: none -> 5.64 us  [shards(): jnp.stack([tail_rows] * lax.axis_size('ctx'))]
where the time goes in v1:
time: 540 us; the launch traced here: 539 us
  waiting for transfers between devices  256 us (47%)
  matrix products  131 us (24%)
  local copies, waits for them, and re-layouts  47.2 us (9%)
  blocking collectives  44.3 us (8%)
  other arithmetic  29.1 us (5%)
  between operations  13.6 us (3%)
  loops' own time  8.67 us (2%)
  starting transfers between devices  8.44 us (2%)
    all_to_all x1, waiting for transfers between devices, shards(): lax.all_to_all(jnp.stack([tail_rows] * lax.axis_size('ctx')), 'ctx', 0, 0)  184 us
    all_gather x1, waiting for transfers between devices, side_by_side(): out = lax.all_gather(both, axis, axis=dim, tiled=True)  71.9 us
    dot_general x12, matrix products, attend_block(): jnp.einsum('hgqk,khd->hgqd', weight.astype(jnp.bfloat16), value_block, pr...  57.8 us
    dot_general x12, matrix products, attend_block(): jnp.einsum('qhgd,khd->hgqk', query_heads, key_block, preferred_element_ty...  57.3 us
    all_to_all x1, blocking collectives, sum_at_owner(): tiles = lax.all_to_all(in_blocks(x, dim, size), axis, 0, 0, tiled=True)  44.3 us
    reduce_sum x12, other arithmetic, attend_block(): row_total = row_total * factor + jnp.sum(weight, axis=-1)  18.6 us
    reshape x1, local copies, waits for them, and re-layouts, shards(): jnp.concatenate(lax.all_to_all(jnp.stack([tail_rows] * lax.axis_size('ctx...  17.8 us
  transfers between devices with their start and end apart: 2, of which 2 were waited for; matrix products, arithmetic and copies ran while one was open for 1% of the time, Pallas kernels for 0%

profile of v1, /device:TPU:1, one launch (start us, length us, event | category | flops | bytes accessed | tf_op | source)
XLA Modules:
  0.0 538.8 jit_solution(17708577920533310635)
XLA Ops:
  10.6 71.9 %all-gather.2.cloned.1.call-done = bf16[12288,256]{1,0:T(8,128)(2,1)} async-done(((bf16[384,256]{1,0:T(8,128)(2,1)}), bf16[12288,256]{1,0:T(8,128)(2,1)}) %all-gather.2.cloned.1.call-update) | async-done | bytes 6291472 | tf_op jit(solution)/shard_map/all_gather | solution.py:14
  87.2 156.6 %while.17 = (s32[]{:T(128)}, f32[1,4,384]{2,1,0:T(4,128)S(1)}, f32[1,4,384]{2,1,0:T(4,128)S(1)}, f32[1,4,384,128]{3,2,1,0:T(8,128)S(1)}, s32[12]{0:T(128)S(1)}, ...) while((s32[]{:T(128)}, f32[1,4,384]{2,1,0:T(4,128)S(1)}, ...), condition=%wide.region_6.7_spmd.clone, body=%wide.region_2.6_spmd.clone.sunk | while | flops 826960256 | bytes 48233928 | solution.py:98
  89.1 4.8 fusion.62
  93.9 4.8 fusion.65
  102.1 4.8 fusion.62
  106.9 4.8 fusion.65
  115.2 4.8 fusion.62
  120.0 4.8 fusion.65
  128.2 4.8 fusion.62
  133.0 4.8 fusion.65
  141.3 4.8 fusion.62
  146.1 4.8 fusion.65
  154.3 4.8 fusion.62
  159.1 4.8 fusion.65
  172.2 4.8 fusion.65
  180.4 4.8 fusion.62
  185.2 4.8 fusion.65
  193.5 4.8 fusion.62
  198.3 4.8 fusion.65
  206.5 4.8 fusion.62
  211.3 4.8 fusion.65
  219.6 4.8 fusion.62
  224.4 4.8 fusion.65
  232.6 4.8 fusion.62
  237.4 4.8 fusion.65
  248.5 44.3 %all_to_all.10 = bf16[8,384,512]{2,1,0:T(8,128)(2,1)S(1)} all-to-all(bf16[8,384,512]{2,1,0:T(8,128)(2,1)S(1)} %bitcast.107), channel_id=1, replica_groups=mesh['ctx'=32,'head'=8] {'head'}, dimensions={0} | all-to-all | bytes 6291456 | tf_op jit(solution)/shard_map/all_to_all | solution.py:26
  293.9 5.6 %stack.2 = bf16[32,2,127,512]{3,1,2,0:T(2,128)(2,1)} broadcast(bf16[2,127,512]{2,0,1:T(2,128)(2,1)S(1)} %copy.50), dimensions={1,2,3} | broadcast | bytes 8583168 | tf_op jit(solution)/shard_map/stack | solution.py:115
  299.5 8.4 %all-to-all-start.1 = ((bf16[32,2,127,512]{3,1,2,0:T(2,128)(2,1)}), bf16[32,2,127,512]{3,1,2,0:T(2,128)(2,1)}, u32[]{:S(2)}, u32[]{:S(2)}) async-start(bf16[32,2,127,512]{3,1,2,0:T(2,128)(2,1)} %stack.2), calls=%async_computation.1 | async-start | bytes 16646144 | tf_op jit(solution)/shard_map/all_to_all | solution.py:115
  308.6 184.4 %all-to-all-done.1 = bf16[32,2,127,512]{3,1,2,0:T(2,128)(2,1)} async-done(((bf16[32,2,127,512]{3,1,2,0:T(2,128)(2,1)}), bf16[32,2,127,512]{3,1,2,0:T(2,128)(2,1)}, u32[]{:S(2)}, u32[]{:S(2)}) %all-to-all-start.1) | async-done | bytes 8323104 | tf_op jit(solution)/shard_map/all_to_all | solution.py:115
  493.0 8.1 %copy.51 = bf16[32,2,127,512]{3,1,0,2:T(2,128)(2,1)} copy(bf16[32,2,127,512]{3,1,2,0:T(2,128)(2,1)} %all-to-all-done.1) | data formatting | bytes 16646144 | tf_op jit(solution)/shard_map/all_to_all | solution.py:115
  501.1 17.8 %reshape.136 = bf16[64,127,512]{2,0,1:T(8,128)(2,1)} reshape(bf16[32,2,127,512]{3,1,0,2:T(2,128)(2,1)} %copy.51) | data formatting | bytes 16646144 | tf_op jit(solution)/shard_map/reshape | solution.py:114
  523.4 7.5 %fusion.34 = f32[2,192,512]{2,0,1:T(2,128)S(1)} fusion(bf16[2,192,512]{2,0,1:T(2,128)(2,1)S(1)} %copy.52, bf16[2,127,512]{2,0,1:T(2,128)(2,1)S(1)} %convolution_convert_fusion.1, f32[128,1,512]{2,0,1:T(8,128)S(1)} %bitcast.119), kind=kOutput, calls=%fused_computation.49 | convolution fusion | flops 303296512 | bytes 1701888 | tf_op jit(solution)/shard_map/conv_general_dilated | solution.py:126
  (190 shorter events, 58.3 us)
Async XLA Ops:
  6.5 75.9 %all-gather.2.cloned.1.call-start = ((), (), s32[]{:S(2)}) async-start(), calls=%async_computation.2 | async-start | bytes 6488064 | tf_op jit(solution)/shard_map/all_gather | solution.py:14
  10.5 76.7 %copy-start.3 = (s32[64]{0:T(128)S(1)}, s32[64]{0:T(128)}, u32[]{:S(2)}) copy-start(s32[64]{0:T(128)} %param.10) | copy-start | bytes 772
  93.9 4.8 copy-start
  106.9 4.8 copy-start
  120.0 4.8 copy-start
  133.0 4.8 copy-start
  146.1 4.8 copy-start
  159.1 4.8 copy-start
  172.2 4.8 copy-start
  185.2 4.8 copy-start
  198.3 4.8 copy-start
  211.3 4.8 copy-start
  224.4 4.8 copy-start
  237.4 4.8 copy-start
  299.5 8.4 %copy-start.2 = (f32[128,512]{1,0:T(8,128)S(1)}, f32[128,512]{1,0:T(8,128)}, u32[]{:S(2)}) copy-start(f32[128,512]{1,0:T(8,128)} %param.15) | copy-start | bytes 786436
  299.5 193.5 %all-to-all-start.1 = ((bf16[32,2,127,512]{3,1,2,0:T(2,128)(2,1)}), bf16[32,2,127,512]{3,1,2,0:T(2,128)(2,1)}, u32[]{:S(2)}, u32[]{:S(2)}) async-start(bf16[32,2,127,512]{3,1,2,0:T(2,128)(2,1)} %stack.2), calls=%async_computation.1 | async-start | bytes 16646144 | tf_op jit(solution)/shard_map/all_to_all | solution.py:115
  523.4 7.5 %copy-start.1 = (bf16[384,512]{1,0:T(8,128)(2,1)S(1)}, bf16[384,512]{1,0:T(8,128)(2,1)}, u32[]{:S(2)}) copy-start(bf16[384,512]{1,0:T(8,128)(2,1)} %param.17) | copy-start | bytes 1179652
  523.4 7.5 %copy-start.4 = (f32[512]{0:T(512)S(1)}, f32[512]{0:T(512)}, u32[]{:S(2)}) copy-start(f32[512]{0:T(512)} %param.16) | copy-start | bytes 6148
Sparse Core Ops, SparseCore 0:
  9.2 73.2 all-gather.1
